TPU v7x, 32 devices: a whole 2x2x4 slice. The times are simulated.
32 devices in a mesh: bin: 4 (over z), row: 2 (over y), col: 4 (over x, core).
Axes of the slice: x: 2, y: 2, z: 4, core: 2. Of those that a mesh axis runs over, the one named last changes fastest.
Arguments:
- responses: bfloat16 [2, 4, 4096, 4096], P(None, 'bin', 'row', 'col'), may hold values from -6 to 6
- focusing: bfloat16 [2, 4, 16, 256, 256], P(None, 'bin', 'row'), may hold values from -0.25 to 0.25
- panel: bfloat16 [2, 4096, 256], P(None, 'col'), may hold values from -0.03125 to 0.03125
Outputs:
- projected: float32 [2, 256, 4096], P(None, 'col', 'row')
All inputs are finite; a program needn't handle non-finite values.
Results may differ from a plain program's by a relative error of at most 0.0041.
Values may be sent and summed in bfloat16 or wider, within the bound.
No kernel may reach another device: no remote copies, remote signals or barrier semaphores. Data moves between devices by JAX's collectives and lax.ppermute only.
A program may use at most 128 MiB of HBM per device.

v0:
```python
import jax
import jax.numpy as jnp
from jax import lax
from jax.sharding import PartitionSpec as P


def left_focus(blk_real, blk_imag, resp_real, resp_imag):

    def product(left_op, right_op):
        return jnp.einsum("fjab,fjbm->fjam", left_op, right_op, preferred_element_type=jnp.float32)

    return (
        product(blk_real, resp_real) - product(blk_imag, resp_imag),
        product(blk_real, resp_imag) + product(blk_imag, resp_real),
    )


def right_focus(left_real, left_imag, blk_real, blk_imag):

    def product(left_op, right_op):
        return jnp.einsum("fnjb,fjab->fnja", left_op, right_op, preferred_element_type=jnp.float32)

    return (
        product(left_real, blk_real) + product(left_imag, blk_imag),
        product(left_imag, blk_real) - product(left_real, blk_imag),
    )


def project_joint(foc_real, foc_imag, pan_real, pan_imag):

    def product(left_op, right_op):
        return jnp.einsum("fnm,mcbs->bcsn", left_op, right_op, preferred_element_type=jnp.float32)

    proj_real = product(foc_real, pan_real) - product(foc_imag, pan_imag)
    proj_imag = product(foc_real, pan_imag) + product(foc_imag, pan_real)
    return (proj_real, proj_imag)


def local(responses, focusing, panel):
    bins_here = responses.shape[1]
    tile_rows = responses.shape[2]
    tile_cols = responses.shape[3]
    row_blocks = focusing.shape[2]
    block_size = focusing.shape[3]
    col_blocks = tile_cols // block_size
    width_k = panel.shape[2]
    col_count = lax.axis_size("col")
    bin_count = lax.axis_size("bin")
    resp_real = responses[0].reshape(bins_here, row_blocks, block_size, tile_cols)
    resp_imag = responses[1].reshape(bins_here, row_blocks, block_size, tile_cols)
    left_real, left_imag = left_focus(focusing[0], focusing[1], resp_real, resp_imag)
    left_real = left_real.reshape(bins_here, tile_rows, col_blocks, block_size).astype(jnp.bfloat16)
    left_imag = left_imag.reshape(bins_here, tile_rows, col_blocks, block_size).astype(jnp.bfloat16)
    first_block = lax.axis_index("col") * col_blocks
    all_blocks = lax.all_gather(focusing, "row", axis=2, tiled=True)
    col_focus = lax.dynamic_slice_in_dim(all_blocks, first_block, col_blocks, 2)
    foc_real, foc_imag = right_focus(left_real, left_imag, col_focus[0], col_focus[1])
    foc_real = foc_real.reshape(bins_here, tile_rows, tile_cols).astype(jnp.bfloat16)
    foc_imag = foc_imag.reshape(bins_here, tile_rows, tile_cols).astype(jnp.bfloat16)
    slice_k = width_k // (col_count * bin_count)
    pan_real = panel[0].reshape(tile_cols, col_count, bin_count, slice_k)
    pan_imag = panel[1].reshape(tile_cols, col_count, bin_count, slice_k)
    proj_real, proj_imag = project_joint(foc_real, foc_imag, pan_real, pan_imag)
    partial_proj = jnp.stack(
        [proj_real.reshape(width_k, tile_rows), proj_imag.reshape(width_k, tile_rows)]
    )
    shared = lax.psum_scatter(partial_proj, ("bin", "col"), scatter_dimension=1, tiled=True)
    result = lax.all_gather(shared, "bin", axis=1, tiled=True)
    return result


def solution(mesh):
    return jax.shard_map(
        local,
        mesh=mesh,
        in_specs=(
            P(None, "bin", "row", "col"),
            P(None, "bin", "row", None, None),
            P(None, "col", None),
        ),
        out_specs=P(None, "col", "row"),
        check_vma=False,
    )
```

profile of v0, /device:TPU:0, one launch (start us, length us, event | category | flops | bytes accessed | tf_op | source)
XLA Modules:
  0.0 199.6 jit_solution(4494952446536381872)
XLA Ops:
  6.5 0.0 all-gather.3.cloned.1.call-start
  6.5 0.7 all-gather.3.cloned.1.call-update
  7.3 0.0 reduce-scatter.2.cloned.1.call-start
  7.3 0.0 copy-start.5
  7.3 4.1 %fusion.32 = (bf16[1,1,2048,1024]{3,2,1,0:T(8,128)(2,1)S(1)}, bf16[1,1,2048,1024]{3,2,1,0:T(8,128)(2,1)S(1)}) fusion(bf16[2,1,2048,1024]{3,2,1,0:T(8,128)(2,1)} %param.3), kind=kLoop, calls=%fused_computation.41 | loop fusion | bytes 16777216 | tf_op jit(solution)/shard_map/slice | solution.py:50
  11.4 0.0 copy-start
  11.4 0.0 copy-start.2
  11.4 0.0 copy-done.5
  11.4 1.3 fusion.10
  12.7 0.7 copy-done
  13.4 1.3 copy-done.2
  14.6 3.2 %subtract_convert_fusion.1 = bf16[8,256,1024]{2,1,0:T(8,128)(2,1)} fusion(f32[8,256,1024]{2,1,0:T(8,128)S(1)} %fusion.10, bf16[8,256,1024]{2,1,0:T(8,128)(2,1)S(1)} %bitcast.70, bf16[2,1,8,256,256]{4,3,2,1,0:T(8,128)(2,1)S(1)} %copy-done.5), kind=kOutput, calls=%fused_computation.3 | convolution fusion | flops 1077936128 | bytes 17825792 | tf_op jit(solution)/shard_map/fjab,fjbm->fjam/dot_general | solution.py:10
  17.9 8.2 %convert_element_type.57 = bf16[2048,4,256]{2,1,0:T(4,128)(2,1)} reshape(bf16[8,256,1024]{2,1,0:T(8,128)(2,1)} %subtract_convert_fusion.1) | data formatting | bytes 8388608 | tf_op jit(solution)/shard_map/convert_element_type | solution.py:52
  26.1 0.0 copy-start.1
  26.1 3.6 %fusion.8 = f32[8,256,1024]{2,1,0:T(8,128)S(1)} fusion(bf16[8,256,1024]{2,1,0:T(8,128)(2,1)} %bitcast.71, bf16[2,1,8,256,256]{4,3,2,1,0:T(8,128)(2,1)S(1)} %copy-done.5), kind=kOutput, calls=%fused_computation.15 | convolution fusion | flops 1073741824 | bytes 13631488 | tf_op jit(solution)/shard_map/fjab,fjbm->fjam/dot_general | solution.py:10
  29.7 0.0 copy-done.1
  29.7 3.2 %add_convert_fusion.1 = bf16[8,256,1024]{2,1,0:T(8,128)(2,1)} fusion(f32[8,256,1024]{2,1,0:T(8,128)S(1)} %fusion.8, bf16[8,256,1024]{2,1,0:T(8,128)(2,1)S(1)} %bitcast.69, bf16[2,1,8,256,256]{4,3,2,1,0:T(8,128)(2,1)S(1)} %copy-done.5), kind=kOutput, calls=%fused_computation.2 | convolution fusion | flops 1077936128 | bytes 17825792 | tf_op jit(solution)/shard_map/fjab,fjbm->fjam/dot_general | solution.py:10
  32.9 7.9 %convert_element_type.59 = bf16[2048,4,256]{2,1,0:T(4,128)(2,1)} reshape(bf16[8,256,1024]{2,1,0:T(8,128)(2,1)} %add_convert_fusion.1) | data formatting | bytes 8388608 | tf_op jit(solution)/shard_map/convert_element_type | solution.py:53
  40.7 27.6 %all-gather.3.cloned.1.call-done = bf16[2,1,16,256,256]{4,3,2,1,0:T(8,128)(2,1)} async-done(((bf16[2,1,8,256,256]{4,3,2,1,0:T(8,128)(2,1)}), bf16[2,1,16,256,256]{4,3,2,1,0:T(8,128)(2,1)}) %all-gather.3.cloned.1.call-update) | async-done | bytes 4194320 | tf_op jit(solution)/shard_map/all_gather | solution.py:55
  68.4 0.0 copy-start.3
  68.4 3.8 %fusion = f32[4,256,2048]{2,1,0:T(8,128)S(1)} fusion(bf16[2048,4,256]{2,1,0:T(4,128)(2,1)} %convert_element_type.59, bf16[2,1,16,256,256]{4,3,2,1,0:T(8,128)(2,1)} %all-gather.3.cloned.1.call-done, s32[]{:T(128)S(6)} %select_n.3), kind=kOutput, calls=%fused_computation.5 | convolution fusion | flops 1073741824 | bytes 13107204 | tf_op jit(solution)/shard_map/fnjb,fjab->fnja/dot_general | solution.py:21
  72.2 0.0 copy-done.3
  72.2 0.0 copy-start.6
  72.2 2.6 %subtract_convert_fusion = bf16[4,256,2048]{2,1,0:T(8,128)(2,1)S(1)} fusion(f32[4,256,2048]{2,1,0:T(8,128)S(1)} %fusion, bf16[2048,4,256]{2,1,0:T(4,128)(2,1)S(1)} %copy-done.3, bf16[2,1,16,256,256]{4,3,2,1,0:T(8,128)(2,1)} %all-gather.3.cloned.1.call-done, s32[]{:T(128)S(6)} %add.25, s32[]{:T(128)S(6)} %select_n.3), kind=kOutput, calls=%fused_computation | convolution fusion | flops 1077936128 | bytes 17301512 | tf_op jit(solution)/shard_map/fnjb,fjab->fnja/dot_general | solution.py:21
  74.8 0.0 copy-start.7
  74.8 0.0 copy-done.6
  74.8 1.3 fusion.18
  76.1 0.0 copy-done.7
  76.1 1.3 fusion.20
  77.4 0.0 copy-start.4
  77.4 2.5 %fusion.4 = f32[4,256,2048]{2,1,0:T(8,128)S(1)} fusion(bf16[2048,4,256]{2,1,0:T(4,128)(2,1)S(1)} %copy-done.3, bf16[2,1,16,256,256]{4,3,2,1,0:T(8,128)(2,1)} %all-gather.3.cloned.1.call-done, s32[]{:T(128)S(6)} %select_n.3), kind=kOutput, calls=%fused_computation.9 | convolution fusion | flops 1073741824 | bytes 13107204 | tf_op jit(solution)/shard_map/fnjb,fjab->fnja/dot_general | solution.py:21
  79.9 0.0 copy-done.4
  79.9 2.5 %add_convert_fusion = bf16[4,256,2048]{2,1,0:T(8,128)(2,1)S(1)} fusion(f32[4,256,2048]{2,1,0:T(8,128)S(1)} %fusion.4, bf16[2048,4,256]{2,1,0:T(4,128)(2,1)S(1)} %copy-done.4, bf16[2,1,16,256,256]{4,3,2,1,0:T(8,128)(2,1)} %all-gather.3.cloned.1.call-done, s32[]{:T(128)S(6)} %add.25, s32[]{:T(128)S(6)} %select_n.3), kind=kOutput, calls=%fused_computation.1 | convolution fusion | flops 1077936128 | bytes 17301512 | tf_op jit(solution)/shard_map/fnjb,fjab->fnja/dot_general | solution.py:21
  82.5 0.0 copy-start.8
  82.5 2.4 %fusion.22 = f32[2048,256]{0,1:S(1)} fusion(bf16[2048,1024]{0,1:T(8,128)(2,1)S(1)} %bitcast.74, bf16[2,1024,256]{2,1,0:T(8,128)(2,1)} %param.5), kind=kOutput, calls=%fused_computation.31 | convolution fusion | flops 1073741824 | bytes 6815744
  84.9 0.0 copy-done.8
  84.9 1.3 fusion.16
  86.2 0.3 add_bitcast_fusion
  86.4 0.1 copy.25
  86.6 0.3 subtract_bitcast_fusion
  86.8 0.1 copy.22
  87.0 2.2 %pad_maximum_fusion = f32[2,256,2048]{2,1,0:T(8,128)} fusion(f32[1,256,2048]{2,1,0:T(8,128)S(1)} %bitcast.72, f32[1,256,2048]{2,1,0:T(8,128)S(1)} %bitcast.73), kind=kLoop, calls=%fused_computation.4 | loop fusion | flops 1048576 | bytes 8388608 | tf_op jit(solution)/shard_map/stack | solution.py:64
  89.2 0.0 reduce-scatter.2.cloned.1.call-update
  89.3 0.0 all-gather.5.cloned.1.call-start
  89.3 72.9 %reduce-scatter.2.cloned.1.call-done = f32[2,16,2048]{2,1,0:T(8,128)} async-done(((f32[2,256,2048]{2,1,0:T(8,128)}), f32[2,16,2048]{2,1,0:T(8,128)}) %reduce-scatter.2.cloned.1.call-update) | async-done | bytes 262160 | tf_op jit(solution)/shard_map/reduce_scatter | solution.py:67
  162.2 0.0 all-gather.5.cloned.1.call-update
  162.2 28.6 %all-gather.5.cloned.1.call-done = f32[2,64,2048]{2,1,0:T(8,128)} async-done(((f32[2,16,2048]{2,1,0:T(8,128)}), f32[2,64,2048]{2,1,0:T(8,128)}) %all-gather.5.cloned.1.call-update) | async-done | bytes 1048592 | tf_op jit(solution)/shard_map/all_gather | solution.py:68
  190.8 2.3 %copy.39 = f32[2,64,2048]{2,1,0:T(8,128)} copy(f32[2,64,2048]{2,1,0:T(8,128)} %all-gather.5.cloned.1.call-done) | data formatting | bytes 2097152
Async XLA Ops:
  6.5 61.8 %all-gather.3.cloned.1.call-start = ((), (), s32[]{:S(2)}) async-start(), calls=%async_computation.1 | async-start | bytes 6291456 | tf_op jit(solution)/shard_map/all_gather | solution.py:55
  7.3 154.9 %reduce-scatter.2.cloned.1.call-start = ((), (), s32[]{:S(2)}) async-start(), calls=%async_computation.2 | async-start | bytes 4456448 | tf_op jit(solution)/shard_map/reduce_scatter | solution.py:67
  7.3 4.1 %copy-start.5 = (bf16[2,1,8,256,256]{4,3,2,1,0:T(8,128)(2,1)S(1)}, bf16[2,1,8,256,256]{4,3,2,1,0:T(8,128)(2,1)}, u32[]{:S(2)}) copy-start(bf16[2,1,8,256,256]{4,3,2,1,0:T(8,128)(2,1)} %param.4) | copy-start | bytes 6291460
  11.4 2.0 copy-start
  11.4 3.2 %copy-start.2 = (bf16[1,1,2048,1024]{3,2,1,0:T(8,128)(2,1)}, bf16[1,1,2048,1024]{3,2,1,0:T(8,128)(2,1)S(1)}, u32[]{:S(2)}) copy-start(bf16[1,1,2048,1024]{3,2,1,0:T(8,128)(2,1)S(1)} %get-tuple-element.5) | copy-start | bytes 12582916
  26.1 3.6 %copy-start.1 = (bf16[1,1,2048,1024]{3,2,1,0:T(8,128)(2,1)S(1)}, bf16[1,1,2048,1024]{3,2,1,0:T(8,128)(2,1)}, u32[]{:S(2)}) copy-start(bf16[1,1,2048,1024]{3,2,1,0:T(8,128)(2,1)} %copy-done) | copy-start | bytes 12582916
  68.4 3.8 %copy-start.3 = (bf16[2048,4,256]{2,1,0:T(4,128)(2,1)S(1)}, bf16[2048,4,256]{2,1,0:T(4,128)(2,1)}, u32[]{:S(2)}) copy-start(bf16[2048,4,256]{2,1,0:T(4,128)(2,1)} %convert_element_type.57) | copy-start | bytes 12582916
  72.2 2.6 %copy-start.6 = (bf16[2,1024,256]{2,1,0:T(8,128)(2,1)S(1)}, bf16[2,1024,256]{2,1,0:T(8,128)(2,1)}, u32[]{:S(2)}) copy-start(bf16[2,1024,256]{2,1,0:T(8,128)(2,1)} %param.5) | copy-start | bytes 3145732
  74.8 1.3 copy-start.7
  77.4 2.5 %copy-start.4 = (bf16[2048,4,256]{2,1,0:T(4,128)(2,1)S(1)}, bf16[2048,4,256]{2,1,0:T(4,128)(2,1)}, u32[]{:S(2)}) copy-start(bf16[2048,4,256]{2,1,0:T(4,128)(2,1)} %convert_element_type.59) | copy-start | bytes 12582916
  82.5 2.4 %copy-start.8 = (bf16[2,1024,256]{2,1,0:T(8,128)(2,1)S(1)}, bf16[2,1024,256]{2,1,0:T(8,128)(2,1)}, u32[]{:S(2)}) copy-start(bf16[2,1024,256]{2,1,0:T(8,128)(2,1)} %param.5) | copy-start | bytes 3145732
  89.3 101.6 %all-gather.5.cloned.1.call-start = ((), (), s32[]{:S(2)}) async-start(), calls=%async_computation.3 | async-start | bytes 1310720 | tf_op jit(solution)/shard_map/all_gather | solution.py:68
Sparse Core Ops, SparseCore 0:
  8.9 59.4 all-gather.2
  89.4 72.7 reduce-scatter.1
  163.8 27.0 all-gather.4
where the time goes:
time: 200 us
  waiting for transfers between devices  130 us (65%)
  matrix products  29 us (14%)
  local copies, waits for them, and re-layouts  24.7 us (12%)
  between operations  13.3 us (7%)
  other arithmetic  2.74 us (1%)
    reduce_scatter x1, waiting for transfers between devices, local(): lax.psum_scatter(partial_proj, ('bin', 'col'), scatter_dimension=1, tiled...  72.9 us
    all_gather x1, waiting for transfers between devices, local(): result = lax.all_gather(shared, 'bin', axis=1, tiled=True)  28.6 us
    all_gather x1, waiting for transfers between devices, local(): all_blocks = lax.all_gather(focusing, 'row', axis=2, tiled=True)  27.6 us
    dot_general x4, matrix products, product(): jnp.einsum('fnjb,fjab->fnja', left_op, right_op, preferred_element_type=j...  11.5 us
    dot_general x4, matrix products, product(): jnp.einsum('fjab,fjbm->fjam', left_op, right_op, preferred_element_type=j...  11.3 us
    convert_element_type x1, local copies, waits for them, and re-layouts, local(): left_real.reshape(bins_here, tile_rows, col_blocks, block_size)  8.18 us
    convert_element_type x1, local copies, waits for them, and re-layouts, local(): left_imag.reshape(bins_here, tile_rows, col_blocks, block_size)  7.88 us
    unnamed x4, matrix products  6.21 us
  transfers between devices with their start and end apart: 3, of which 3 were waited for; matrix products, arithmetic and copies ran while one was open for 16% of the time, Pallas kernels for 0%

commit v1 on v0

--- a/solution.py
+++ b/solution.py
@@ -52,7 +52,14 @@
     left_real = left_real.reshape(bins_here, tile_rows, col_blocks, block_size).astype(jnp.bfloat16)
     left_imag = left_imag.reshape(bins_here, tile_rows, col_blocks, block_size).astype(jnp.bfloat16)
     first_block = lax.axis_index("col") * col_blocks
-    all_blocks = lax.all_gather(focusing, "row", axis=2, tiled=True)
+    ways, here, step = (lax.axis_size("row"), lax.axis_index("row"), focusing.shape[2])
+    line, have = (focusing, 1)
+    while have < ways:
+        line = jnp.concatenate(
+            [line, lax.ppermute(line, "row", [(d, (d - have) % ways) for d in range(ways)])], axis=2
+        )
+        have = 2 * have
+    all_blocks = jnp.roll(line, here * step, axis=2)
     col_focus = lax.dynamic_slice_in_dim(all_blocks, first_block, col_blocks, 2)
     foc_real, foc_imag = right_focus(left_real, left_imag, col_focus[0], col_focus[1])
     foc_real = foc_real.reshape(bins_here, tile_rows, tile_cols).astype(jnp.bfloat16)

time: 200 us -> 191 us (0.955)
  waiting for transfers between devices: 130 us -> 109 us
  matrix products: 29 us -> 36.7 us
  starting transfers between devices: 0.08 us -> 3.04 us
    all_gather x1 -> x0, waiting for transfers between devices: 27.6 us -> none  [local(): all_blocks = lax.all_gather(focusing, 'row', axis=2, tiled=True)]
    dot_general x4, matrix products: 11.3 us -> 19.2 us  [product(): jnp.einsum('fjab,fjbm->fjam', left_op, right_op, preferred_element_type=j...]
    ppermute x0 -> x1, waiting for transfers between devices: none -> 5.86 us  [local(): lax.ppermute(line, 'row', [(d, (d - have) % ways) for d in range(ways)])]
    dot_general x4, matrix products: 11.5 us -> 7.51 us  [product(): jnp.einsum('fnjb,fjab->fnja', left_op, right_op, preferred_element_type=j...]
    unnamed x4, matrix products: 6.21 us -> 10 us
    ppermute x0 -> x1, starting transfers between devices: none -> 3 us  [local(): lax.ppermute(line, 'row', [(d, (d - have) % ways) for d in range(ways)])]
  transfers between devices with their start and end apart: 3 -> 3, of which waited for: 3 -> 3; matrix products, arithmetic and copies ran while one was open for 16% -> 21% of each run, Pallas kernels for 0% -> 0%
where the time goes in v1:
time: 191 us
  waiting for transfers between devices  109 us (57%)
  matrix products  36.7 us (19%)
  local copies, waits for them, and re-layouts  24.9 us (13%)
  between operations  13.5 us (7%)
  other arithmetic  3.51 us (2%)
  starting transfers between devices  3.04 us (2%)
    reduce_scatter x1, waiting for transfers between devices, local(): lax.psum_scatter(partial_proj, ('bin', 'col'), scatter_dimension=1, tiled...  74.6 us
    all_gather x1, waiting for transfers between devices, local(): result = lax.all_gather(shared, 'bin', axis=1, tiled=True)  28.6 us
    dot_general x4, matrix products, product(): jnp.einsum('fjab,fjbm->fjam', left_op, right_op, preferred_element_type=j...  19.2 us
    unnamed x4, matrix products  10 us
    convert_element_type x1, local copies, waits for them, and re-layouts, local(): left_real.reshape(bins_here, tile_rows, col_blocks, block_size)  7.87 us
    convert_element_type x1, local copies, waits for them, and re-layouts, local(): left_imag.reshape(bins_here, tile_rows, col_blocks, block_size)  7.82 us
    dot_general x4, matrix products, product(): jnp.einsum('fnjb,fjab->fnja', left_op, right_op, preferred_element_type=j...  7.51 us
    ppermute x1, waiting for transfers between devices, local(): lax.ppermute(line, 'row', [(d, (d - have) % ways) for d in range(ways)])  5.86 us
  transfers between devices with their start and end apart: 3, of which 3 were waited for; matrix products, arithmetic and copies ran while one was open for 21% of the time, Pallas kernels for 0%

profile of v1, /device:TPU:0, one launch (start us, length us, event | category | flops | bytes accessed | tf_op | source)
XLA Modules:
  0.0 190.7 jit_solution(13497556214604273211)
XLA Ops:
  6.5 0.0 copy-start.4
  6.5 0.0 reduce-scatter.2.cloned.1.call-start
  6.5 3.0 %collective-permute-start = (bf16[2,1,8,256,256]{4,3,2,1,0:T(8,128)(2,1)}, bf16[2,1,8,256,256]{4,3,2,1,0:T(8,128)(2,1)}, u32[]{:S(2)}, u32[]{:S(2)}) collective-permute-start(bf16[2,1,8,256,256]{4,3,2,1,0:T(8,128)(2,1)} %param.4), channel_id=1, source_target_pairs={{0,4},{4,0},{1,5},{5,1},{2,6},{6,2},{3,7},{7,3},{8,12},{12,8},{9,1... | collective-permute-start | bytes 6291464 | tf_op jit(solution)/shard_map/ppermute | solution.py:59
  9.5 5.2 %fusion.31 = (bf16[1,1,2048,1024]{3,2,1,0:T(8,128)(2,1)}, bf16[1,1,2048,1024]{3,2,1,0:T(8,128)(2,1)S(1)}) fusion(bf16[2,1,2048,1024]{3,2,1,0:T(8,128)(2,1)} %param.3), kind=kLoop, calls=%fused_computation.44 | loop fusion | bytes 16777216 | tf_op jit(solution)/shard_map/slice | solution.py:49
  14.8 0.0 copy-start
  14.8 0.0 copy-done.4
  14.8 4.5 %fusion.11 = f32[8,256,1024]{2,1,0:T(8,128)} fusion(bf16[8,256,1024]{2,1,0:T(8,128)(2,1)S(1)} %bitcast.68, bf16[2,1,8,256,256]{4,3,2,1,0:T(8,128)(2,1)S(1)} %copy-done.4), kind=kOutput, calls=%fused_computation.22 | convolution fusion | flops 1073741824 | bytes 13631488 | tf_op jit(solution)/shard_map/fjab,fjbm->fjam/dot_general | solution.py:10
  19.3 0.0 copy-done
  19.3 7.9 %add_convert_fusion.1 = bf16[8,256,1024]{2,1,0:T(8,128)(2,1)} fusion(f32[8,256,1024]{2,1,0:T(8,128)} %fusion.11, bf16[8,256,1024]{2,1,0:T(8,128)(2,1)} %bitcast.70, bf16[2,1,8,256,256]{4,3,2,1,0:T(8,128)(2,1)S(1)} %copy-done.4), kind=kOutput, calls=%fused_computation.6 | convolution fusion | flops 1077936128 | bytes 17825792 | tf_op jit(solution)/shard_map/fjab,fjbm->fjam/dot_general | solution.py:10
  27.1 7.8 %convert_element_type.59 = bf16[2048,4,256]{2,1,0:T(4,128)(2,1)} reshape(bf16[8,256,1024]{2,1,0:T(8,128)(2,1)} %add_convert_fusion.1) | data formatting | bytes 8388608 | tf_op jit(solution)/shard_map/convert_element_type | solution.py:53
  35.0 0.0 copy-start.1
  35.0 3.6 %fusion.13 = f32[8,256,1024]{2,1,0:T(8,128)S(1)} fusion(bf16[8,256,1024]{2,1,0:T(8,128)(2,1)} %bitcast.71, bf16[2,1,8,256,256]{4,3,2,1,0:T(8,128)(2,1)S(1)} %copy-done.4), kind=kOutput, calls=%fused_computation.24 | convolution fusion | flops 1073741824 | bytes 13631488 | tf_op jit(solution)/shard_map/fjab,fjbm->fjam/dot_general | solution.py:10
  38.6 0.0 copy-done.1
  38.6 3.2 %subtract_convert_fusion.1 = bf16[8,256,1024]{2,1,0:T(8,128)(2,1)} fusion(f32[8,256,1024]{2,1,0:T(8,128)S(1)} %fusion.13, bf16[8,256,1024]{2,1,0:T(8,128)(2,1)S(1)} %bitcast.69, bf16[2,1,8,256,256]{4,3,2,1,0:T(8,128)(2,1)S(1)} %copy-done.4), kind=kOutput, calls=%fused_computation.7 | convolution fusion | flops 1077936128 | bytes 17825792 | tf_op jit(solution)/shard_map/fjab,fjbm->fjam/dot_general | solution.py:10
  41.8 7.9 %convert_element_type.57 = bf16[2048,4,256]{2,1,0:T(4,128)(2,1)} reshape(bf16[8,256,1024]{2,1,0:T(8,128)(2,1)} %subtract_convert_fusion.1) | data formatting | bytes 8388608 | tf_op jit(solution)/shard_map/convert_element_type | solution.py:52
  49.7 0.0 copy-start.3
  49.7 5.9 %collective-permute-done = bf16[2,1,8,256,256]{4,3,2,1,0:T(8,128)(2,1)} collective-permute-done((bf16[2,1,8,256,256]{4,3,2,1,0:T(8,128)(2,1)}, bf16[2,1,8,256,256]{4,3,2,1,0:T(8,128)(2,1)}, u32[]{:S(2)}, u32[]{:S(2)}) %collective-permute-start) | collective-permute-done | bytes 2097184 | tf_op jit(solution)/shard_map/ppermute | solution.py:59
  55.5 0.8 fusion.8
  56.3 0.0 copy-done.3
  56.3 0.0 copy-start.2
  56.4 1.3 fusion.3
  57.7 0.9 copy-done.2
  58.5 3.4 %subtract_convert_fusion = bf16[4,256,2048]{2,1,0:T(8,128)(2,1)} fusion(f32[4,256,2048]{2,1,0:T(8,128)S(1)} %fusion.3, bf16[2048,4,256]{2,1,0:T(4,128)(2,1)S(1)} %copy-done.2, bf16[2,1,4,256,256]{4,3,2,1,0:T(8,128)(2,1)S(1)} %fusion.8), kind=kOutput, calls=%fused_computation.4 | convolution fusion | flops 1077936128 | bytes 17301504 | tf_op jit(solution)/shard_map/fnjb,fjab->fnja/dot_general | solution.py:21
  62.0 0.0 copy-start.5
  62.0 0.0 copy-start.7
  62.0 3.8 %fusion.21 = f32[2048,256]{0,1:S(1)} fusion(bf16[2048,1024]{0,1:T(8,128)(2,1)} %bitcast.76, bf16[2,1024,256]{2,1,0:T(8,128)(2,1)} %param.5), kind=kOutput, calls=%fused_computation.34 | convolution fusion | flops 1073741824 | bytes 6815744
  65.7 0.0 copy-done.5
  65.7 0.1 copy-done.7
  65.9 2.6 %fusion.23 = f32[2048,256]{0,1} fusion(bf16[2048,1024]{0,1:T(8,128)(2,1)S(1)} %bitcast.77, bf16[2,1024,256]{2,1,0:T(8,128)(2,1)S(1)} %copy-done.7), kind=kOutput, calls=%fused_computation.36 | convolution fusion | flops 1073741824 | bytes 6815744
  68.5 1.3 fusion.1
  69.8 1.5 add_convert_fusion
  71.3 0.0 copy-start.8
  71.3 2.4 %fusion.25 = f32[2048,256]{0,1:S(1)} fusion(bf16[2048,1024]{0,1:T(8,128)(2,1)S(1)} %bitcast.74, bf16[2,1024,256]{2,1,0:T(8,128)(2,1)} %param.5), kind=kOutput, calls=%fused_computation.38 | convolution fusion | flops 1073741824 | bytes 6815744
  73.7 0.0 copy-done.8
  73.7 0.0 copy-start.6
  73.7 1.3 fusion.19
  75.0 0.3 copy-done.6
  75.3 0.2 add_bitcast_fusion
  75.6 0.1 copy.25
  75.7 0.3 subtract_bitcast_fusion
  76.0 0.1 copy.22
  76.1 2.2 %pad_maximum_fusion = f32[2,256,2048]{2,1,0:T(8,128)} fusion(f32[1,256,2048]{2,1,0:T(8,128)S(1)} %bitcast.72, f32[1,256,2048]{2,1,0:T(8,128)S(1)} %bitcast.73), kind=kLoop, calls=%fused_computation.8 | loop fusion | flops 1048576 | bytes 8388608 | tf_op jit(solution)/shard_map/stack | solution.py:71
  78.3 0.0 reduce-scatter.2.cloned.1.call-update
  78.4 0.0 all-gather.2.cloned.1.call-start
  78.4 74.6 %reduce-scatter.2.cloned.1.call-done = f32[2,16,2048]{2,1,0:T(8,128)} async-done(((f32[2,256,2048]{2,1,0:T(8,128)}), f32[2,16,2048]{2,1,0:T(8,128)}) %reduce-scatter.2.cloned.1.call-update) | async-done | bytes 262160 | tf_op jit(solution)/shard_map/reduce_scatter | solution.py:74
  153.0 0.0 all-gather.2.cloned.1.call-update
  153.0 28.6 %all-gather.2.cloned.1.call-done = f32[2,64,2048]{2,1,0:T(8,128)} async-done(((f32[2,16,2048]{2,1,0:T(8,128)}), f32[2,64,2048]{2,1,0:T(8,128)}) %all-gather.2.cloned.1.call-update) | async-done | bytes 1048592 | tf_op jit(solution)/shard_map/all_gather | solution.py:75
  181.6 2.3 %copy.39 = f32[2,64,2048]{2,1,0:T(8,128)} copy(f32[2,64,2048]{2,1,0:T(8,128)} %all-gather.2.cloned.1.call-done) | data formatting | bytes 2097152
Async XLA Ops:
  6.5 8.2 %copy-start.4 = (bf16[2,1,8,256,256]{4,3,2,1,0:T(8,128)(2,1)S(1)}, bf16[2,1,8,256,256]{4,3,2,1,0:T(8,128)(2,1)}, u32[]{:S(2)}) copy-start(bf16[2,1,8,256,256]{4,3,2,1,0:T(8,128)(2,1)} %param.4) | copy-start | bytes 6291460
  6.5 146.5 %reduce-scatter.2.cloned.1.call-start = ((), (), s32[]{:S(2)}) async-start(), calls=%async_computation.1 | async-start | bytes 4456448 | tf_op jit(solution)/shard_map/reduce_scatter | solution.py:74
  6.5 49.0 %collective-permute-start = (bf16[2,1,8,256,256]{4,3,2,1,0:T(8,128)(2,1)}, bf16[2,1,8,256,256]{4,3,2,1,0:T(8,128)(2,1)}, u32[]{:S(2)}, u32[]{:S(2)}) collective-permute-start(bf16[2,1,8,256,256]{4,3,2,1,0:T(8,128)(2,1)} %param.4), channel_id=1, source_target_pairs={{0,4},{4,0},{1,5},{5,1},{2,6},{6,2},{3,7},{7,3},{8,12},{12,8},{9,1... | collective-permute-start | bytes 6291464 | tf_op jit(solution)/shard_map/ppermute | solution.py:59
  14.8 4.5 %copy-start = (bf16[1,1,2048,1024]{3,2,1,0:T(8,128)(2,1)}, bf16[1,1,2048,1024]{3,2,1,0:T(8,128)(2,1)S(1)}, u32[]{:S(2)}) copy-start(bf16[1,1,2048,1024]{3,2,1,0:T(8,128)(2,1)S(1)} %get-tuple-element.6) | copy-start | bytes 12582916
  35.0 3.6 %copy-start.1 = (bf16[1,1,2048,1024]{3,2,1,0:T(8,128)(2,1)S(1)}, bf16[1,1,2048,1024]{3,2,1,0:T(8,128)(2,1)}, u32[]{:S(2)}) copy-start(bf16[1,1,2048,1024]{3,2,1,0:T(8,128)(2,1)} %copy-done) | copy-start | bytes 12582916
  49.7 6.7 %copy-start.3 = (bf16[2048,4,256]{2,1,0:T(4,128)(2,1)S(1)}, bf16[2048,4,256]{2,1,0:T(4,128)(2,1)}, u32[]{:S(2)}) copy-start(bf16[2048,4,256]{2,1,0:T(4,128)(2,1)} %convert_element_type.57) | copy-start | bytes 12582916
  56.3 2.2 %copy-start.2 = (bf16[2048,4,256]{2,1,0:T(4,128)(2,1)S(1)}, bf16[2048,4,256]{2,1,0:T(4,128)(2,1)}, u32[]{:S(2)}) copy-start(bf16[2048,4,256]{2,1,0:T(4,128)(2,1)} %convert_element_type.59) | copy-start | bytes 12582916
  62.0 3.8 %copy-start.5 = (bf16[4,256,2048]{2,1,0:T(8,128)(2,1)S(1)}, bf16[4,256,2048]{2,1,0:T(8,128)(2,1)}, u32[]{:S(2)}) copy-start(bf16[4,256,2048]{2,1,0:T(8,128)(2,1)} %subtract_convert_fusion) | copy-start | bytes 12582916
  62.0 3.9 %copy-start.7 = (bf16[2,1024,256]{2,1,0:T(8,128)(2,1)S(1)}, bf16[2,1024,256]{2,1,0:T(8,128)(2,1)}, u32[]{:S(2)}) copy-start(bf16[2,1024,256]{2,1,0:T(8,128)(2,1)} %param.5) | copy-start | bytes 3145732
  71.3 2.4 %copy-start.8 = (bf16[2,1024,256]{2,1,0:T(8,128)(2,1)S(1)}, bf16[2,1024,256]{2,1,0:T(8,128)(2,1)}, u32[]{:S(2)}) copy-start(bf16[2,1024,256]{2,1,0:T(8,128)(2,1)} %param.5) | copy-start | bytes 3145732
  73.7 1.6 copy-start.6
  78.4 103.2 %all-gather.2.cloned.1.call-start = ((), (), s32[]{:S(2)}) async-start(), calls=%async_computation.2 | async-start | bytes 1310720 | tf_op jit(solution)/shard_map/all_gather | solution.py:75
Sparse Core Ops, SparseCore 0:
  78.5 74.4 reduce-scatter.1
  154.6 26.9 all-gather.1
